TPU v7x, 32 devices: a whole 2x2x4 slice. The times are simulated.
32 devices in a mesh: seq: 8 (over z, y), head: 4 (over x, core).
Axes of the slice: x: 2, y: 2, z: 4, core: 2. Of those that a mesh axis runs over, the one named last changes fastest.
Arguments:
- block_in: bfloat16 [1, 2048, 1024], P(None, 'seq'), may hold values from -6 to 6
- upstream: bfloat16 [1, 2048, 1024], P(None, 'seq'), may hold values from -6 to 6
- first_gain: float32 [1024], replicated, may hold values from 0.5 to 1.5
- project_in: bfloat16 [1024, 4, 512], P(None, 'head'), may hold values from -0.1875 to 0.1875
- filter_taps: float32 [4, 4, 512], P(None, 'head'), may hold values from -2 to 2
- squeeze: bfloat16 [1024, 16], replicated, may hold values from -0.1875 to 0.1875
- expand: bfloat16 [16, 512], P(None, 'head'), may hold values from -0.75 to 0.75
- decay_bias: float32 [512], P('head'), may hold values from 0 to 16
- gating: bfloat16 [1024, 1024], P(None, 'head'), may hold values from -0.1875 to 0.1875
- head_scale: float32 [256], replicated, may hold values from 0.5 to 1.5
- project_out: bfloat16 [1024, 1024], P('head'), may hold values from -0.375 to 0.375
- second_gain: float32 [1024], replicated, may hold values from 0.5 to 1.5
- hidden_gate: bfloat16 [1024, 2816], P(None, 'head'), may hold values from -0.1875 to 0.1875
- hidden_lift: bfloat16 [1024, 2816], P(None, 'head'), may hold values from -0.1875 to 0.1875
- hidden_drop: bfloat16 [2816, 1024], P('head'), may hold values from -0.15625 to 0.15625
Outputs:
- block_out: bfloat16 [1, 2048, 1024], P(None, 'seq')
- input_grad: float32 [1, 2048, 1024], P(None, 'seq')
- grad_first: float32 [1024], replicated
- grad_project: float32 [1024, 4, 512], P('seq', 'head')
- grad_taps: float32 [4, 4, 512], P(None, 'head')
- grad_squeeze: float32 [1024, 16], replicated
- grad_expand: float32 [16, 512], P(None, 'head')
- grad_bias: float32 [512], P('head')
- grad_gating: float32 [1024, 1024], P('seq', 'head')
- grad_scale: float32 [256], replicated
- grad_output: float32 [1024, 1024], P('head', 'seq')
- grad_second: float32 [1024], replicated
- grad_gate: float32 [1024, 2816], P('seq', 'head')
- grad_lift: float32 [1024, 2816], P('seq', 'head')
- grad_drop: float32 [2816, 1024], P('head', 'seq')
All inputs are finite; a program needn't handle non-finite values.
Results may differ from a plain program's by a relative error of at most 0.02.
Values sent between devices are 32-bit elements; how exact they have to be, the bound alone decides.
A program may use at most 128 MiB of HBM per device.

v0:
```python
import jax
import jax.numpy as jnp
from jax import lax
from jax.sharding import PartitionSpec as P

GROUP = 64
EPS = 1e-05
NORMALIZER = 16.0
HIGH = lax.Precision.HIGHEST


def shifted(x, axis, by):
    size = lax.axis_size(axis)
    pairs = [(i, i + by) for i in range(size) if 0 <= i + by < size]
    return lax.ppermute(x, axis, pairs)


def entering(value, axis, join, neutral, backward):
    count, mine = (lax.axis_size(axis), lax.axis_index(axis))
    pieces = jax.tree.map(lambda part: lax.all_gather(part, axis), value)
    if backward:
        pieces = jax.tree.map(lambda part: part[::-1], pieces)
        mine = count - 1 - mine
    total = jax.tree.map(
        lambda part, zero: jnp.full_like(part, 0) + jnp.asarray(zero, part.dtype), value, neutral
    )

    def lap(position, total):
        longer = join(total, jax.tree.map(lambda part: part[position], pieces))
        return jax.tree.map(lambda new, old: jnp.where(position < mine, new, old), longer, total)

    return lax.fori_loop(0, count - 1, lap, total)


def product(left, right):
    return jnp.dot(left, right, preferred_element_type=jnp.float32)


def against(left, right):
    return lax.dot_general(
        left, right, (((1,), (1,)), ((), ())), preferred_element_type=jnp.float32
    )


def across(left, right):
    return lax.dot_general(
        left, right, (((0,), (0,)), ((), ())), preferred_element_type=jnp.float32
    )


def rms_scale(values):
    return lax.rsqrt(jnp.mean(values * values, axis=-1, keepdims=True) + EPS)


def rms_back(values, scale, gain, incoming):
    weighted = gain * incoming
    cube = scale * scale * scale
    return scale * weighted - values * cube * jnp.mean(values * weighted, axis=-1, keepdims=True)


def silu_grad(values):
    logistic = jax.nn.sigmoid(values)
    return logistic * (1.0 + values * (1.0 - logistic))


def causal_mask(size):
    rows = lax.broadcasted_iota(jnp.int32, (size, size), 0)
    columns = lax.broadcasted_iota(jnp.int32, (size, size), 1)
    return (columns <= rows).astype(jnp.float32)


def chain(earlier, later):
    return (earlier[0] * later[0], later[0][..., None] * earlier[1] + later[1])


def grouped(array, seqs, count):
    return array.reshape((seqs, count, GROUP) + array.shape[2:])


def local_states(decays, updates, backward):

    def step(carry, item):
        decay, update = item
        return (jnp.exp(decay)[..., None] * carry + update, carry)

    init = jnp.zeros_like(updates[:, 0])
    total, states = lax.scan(
        step, init, (jnp.moveaxis(decays, 1, 0), jnp.moveaxis(updates, 1, 0)), reverse=backward
    )
    return (jnp.moveaxis(states, 0, 1), total)


def body(
    block_in,
    upstream,
    first_gain,
    project_in,
    filter_taps,
    squeeze,
    expand,
    decay_bias,
    gating,
    head_scale,
    project_out,
    second_gain,
    hidden_gate,
    hidden_lift,
    hidden_drop,
):
    seqs, tokens, width = block_in.shape
    total_rows = seqs * tokens
    key_dim = expand.shape[1]
    value_dim = gating.shape[1]
    mixed_dim = project_in.shape[2]
    lags = filter_taps.shape[0] - 1
    count = tokens // GROUP
    taps = filter_taps.reshape(lags + 1, mixed_dim)
    weight_in = project_in.reshape(width, mixed_dim)
    residual_in = block_in.reshape(total_rows, width).astype(jnp.float32)
    scale_one = rms_scale(residual_in)
    normed_one = (residual_in * scale_one * first_gain).astype(jnp.bfloat16)
    projected = product(normed_one, weight_in).reshape(seqs, tokens, mixed_dim)
    before = shifted(projected[:, tokens - lags :], "seq", 1)
    padded = jnp.concatenate([before, projected], axis=1)
    filtered = taps[0] * projected
    for lag in range(1, lags + 1):
        filtered = filtered + taps[lag] * padded[:, lags - lag : lags - lag + tokens]
    activated_low = jax.nn.silu(filtered).astype(jnp.bfloat16)
    activated = lax.optimization_barrier(activated_low).astype(jnp.float32)
    root = key_dim ** (-0.5)
    query = grouped(activated[..., :key_dim] * root, seqs, count)
    keys = grouped(activated[..., key_dim : 2 * key_dim], seqs, count)
    values = grouped(activated[..., 2 * key_dim :], seqs, count)
    squeezed = product(normed_one, squeeze).astype(jnp.bfloat16)
    logits = product(squeezed, expand) + decay_bias
    log_decay = grouped(
        (jax.nn.log_sigmoid(logits) / NORMALIZER).reshape(seqs, tokens, key_dim), seqs, count
    )
    gate_in = product(normed_one, gating)
    mask = causal_mask(GROUP)
    running = jnp.einsum("ij,snjc->snic", mask, log_decay, precision=HIGH)
    last = running[:, :, -1]
    query_in = query * jnp.exp(running)
    key_in = keys * jnp.exp(-running)
    key_end = keys * jnp.exp(last[:, :, None] - running)
    scores = jnp.einsum("snic,snjc->snij", query_in, key_in, precision=HIGH) * mask
    updates = jnp.einsum("snjc,snjd->sncd", key_end, values, precision=HIGH)
    starts_zero, state_total = local_states(last, updates, False)
    decay_sum = jnp.sum(last, axis=1)
    decay_total = jnp.exp(decay_sum)
    identity = (jnp.ones_like(decay_total), jnp.zeros_like(state_total))
    incoming = entering((decay_total, state_total), "seq", chain, identity, False)[1]
    before_group = jnp.cumsum(last, axis=1) - last
    starts = starts_zero + jnp.exp(before_group)[..., None] * incoming[:, None]
    mixed = jnp.einsum("snij,snjd->snid", scores, values, precision=HIGH)
    mixed = mixed + jnp.einsum("snic,sncd->snid", query_in, starts, precision=HIGH)
    mixed = mixed.reshape(total_rows, value_dim)
    scale_head = rms_scale(mixed)
    normed_head = mixed * scale_head * head_scale
    gated = (normed_head * jax.nn.silu(gate_in)).astype(jnp.bfloat16)
    branch = lax.psum(product(gated, project_out), "head")
    residual = residual_in + branch
    scale_two = rms_scale(residual)
    normed_two = (residual * scale_two * second_gain).astype(jnp.bfloat16)
    gate_value = product(normed_two, hidden_gate)
    lift_value = product(normed_two, hidden_lift)
    inner = (jax.nn.silu(gate_value) * lift_value).astype(jnp.bfloat16)
    feed = lax.psum(product(inner, hidden_drop), "head")
    block_out = (residual + feed).astype(jnp.bfloat16).reshape(seqs, tokens, width)
    seed = upstream.reshape(total_rows, width)
    grad_drop = across(inner, seed)
    grad_inner = against(seed, hidden_drop)
    grad_gv = (grad_inner * lift_value * silu_grad(gate_value)).astype(jnp.bfloat16)
    grad_lv = (grad_inner * jax.nn.silu(gate_value)).astype(jnp.bfloat16)
    grad_gate = across(normed_two, grad_gv)
    grad_lift = across(normed_two, grad_lv)
    feed_grads = (
        lax.psum_scatter(grad_gate, "seq", scatter_dimension=0, tiled=True),
        lax.psum_scatter(grad_lift, "seq", scatter_dimension=0, tiled=True),
        lax.psum_scatter(grad_drop, "seq", scatter_dimension=1, tiled=True),
    )
    grad_two = lax.psum(against(grad_gv, hidden_gate) + against(grad_lv, hidden_lift), "head")
    grad_second = jnp.sum(grad_two * residual * scale_two, axis=0)
    grad_resid = seed.astype(jnp.float32) + rms_back(residual, scale_two, second_gain, grad_two)
    resid_low = grad_resid.astype(jnp.bfloat16)
    grad_output = across(gated, resid_low)
    grad_gated = against(resid_low, project_out)
    grad_gatein = (grad_gated * normed_head * silu_grad(gate_in)).astype(jnp.bfloat16)
    grad_normhead = grad_gated * jax.nn.silu(gate_in)
    grad_scale = jnp.sum(grad_normhead * mixed * scale_head, axis=0)
    grad_mixed_low = rms_back(mixed, scale_head, head_scale, grad_normhead).astype(jnp.bfloat16)
    grad_mixed = lax.optimization_barrier(grad_mixed_low).astype(jnp.float32)
    outgrad = grouped(grad_mixed.reshape(seqs, tokens, value_dim), seqs, count)
    query_end = jnp.einsum("snic,snid->sncd", query_in, outgrad, precision=HIGH)
    following_zero, back_total = local_states(last, query_end, True)
    after = entering((decay_total, back_total), "seq", chain, identity, True)[1]
    after_group = decay_sum[:, None] - jnp.cumsum(last, axis=1)
    following = following_zero + jnp.exp(after_group)[..., None] * after[:, None]
    inner_group = jnp.einsum("snid,snjd->snij", outgrad, values, precision=HIGH) * mask
    grad_query = jnp.exp(running) * (
        jnp.einsum("snij,snjc->snic", inner_group, key_in, precision=HIGH)
        + jnp.einsum("snid,sncd->snic", outgrad, starts, precision=HIGH)
    )
    grad_keys = jnp.exp(-running) * jnp.einsum(
        "snij,snic->snjc", inner_group, query_in, precision=HIGH
    )
    grad_keys = grad_keys + jnp.exp(last[:, :, None] - running) * jnp.einsum(
        "snjd,sncd->snjc", values, following, precision=HIGH
    )
    grad_values = jnp.einsum("snij,snid->snjd", scores, outgrad, precision=HIGH)
    grad_values = grad_values + jnp.einsum("snjc,sncd->snjd", key_end, following, precision=HIGH)
    grad_running = (query * grad_query - keys * grad_keys).reshape(seqs, tokens, key_dim)
    state_end = decay_total[..., None] * incoming + state_total
    beyond = jnp.sum(state_end * after, axis=-1)
    upper = jnp.transpose(causal_mask(tokens))
    suffix = jnp.einsum("ij,sjc->sic", upper, grad_running, precision=HIGH)
    grad_log = suffix + beyond[:, None]
    grad_act = jnp.concatenate(
        [
            grad_query.reshape(seqs, tokens, key_dim) * root,
            grad_keys.reshape(seqs, tokens, key_dim),
            grad_values.reshape(seqs, tokens, value_dim),
        ],
        axis=-1,
    )
    grad_filtered = grad_act * silu_grad(filtered)
    later = shifted(grad_filtered[:, :lags], "seq", -1)
    padded_back = jnp.concatenate([grad_filtered, later], axis=1)
    grad_projected = taps[0] * grad_filtered
    tap_rows = [jnp.sum(grad_filtered * projected, axis=(0, 1))]
    for lag in range(1, lags + 1):
        grad_projected = grad_projected + taps[lag] * padded_back[:, lag : lag + tokens]
        tap_rows.append(
            jnp.sum(grad_filtered * padded[:, lags - lag : lags - lag + tokens], axis=(0, 1))
        )
    grad_taps = jnp.stack(tap_rows).reshape(lags + 1, 1, mixed_dim)
    grad_projected = grad_projected.reshape(total_rows, mixed_dim).astype(jnp.bfloat16)
    grad_logits = grad_log.reshape(total_rows, key_dim) * jax.nn.sigmoid(-logits) / NORMALIZER
    grad_bias = jnp.sum(grad_logits, axis=0)
    logits_low = grad_logits.astype(jnp.bfloat16)
    grad_expand = across(squeezed, logits_low)
    squeeze_low = against(logits_low, expand).astype(jnp.bfloat16)
    grad_squeeze = across(normed_one, squeeze_low)
    grad_project = across(normed_one, grad_projected).reshape(width, 1, mixed_dim)
    grad_gating = across(normed_one, grad_gatein)
    partial_value = (
        against(grad_projected, weight_in)
        + against(grad_gatein, gating)
        + against(squeeze_low, squeeze)
    )
    grad_one = lax.psum(partial_value, "head")
    grad_first = jnp.sum(grad_one * residual_in * scale_one, axis=0)
    input_grad = (grad_resid + rms_back(residual_in, scale_one, first_gain, grad_one)).reshape(
        seqs, tokens, width
    )
    mixer_grads = (
        lax.psum_scatter(grad_project, "seq", scatter_dimension=0, tiled=True),
        lax.psum_scatter(grad_gating, "seq", scatter_dimension=0, tiled=True),
        lax.psum_scatter(grad_output, "seq", scatter_dimension=1, tiled=True),
    )
    summed = tuple(mixer_grads) + tuple(feed_grads)
    small_head = lax.psum((grad_taps, grad_expand, grad_bias, grad_first, grad_second), "seq")
    shared = lax.psum((grad_scale, grad_squeeze), ("seq", "head"))
    return (
        block_out,
        input_grad,
        small_head[3],
        summed[0],
        small_head[0],
        shared[1],
        small_head[1],
        small_head[2],
        summed[1],
        shared[0],
        summed[2],
        small_head[4],
        summed[3],
        summed[4],
        summed[5],
    )


def solution(mesh):
    in_specs = (
        P(None, "seq", None),
        P(None, "seq", None),
        P(),
        P(None, "head", None),
        P(None, "head", None),
        P(),
        P(None, "head"),
        P("head"),
        P(None, "head"),
        P(),
        P("head", None),
        P(),
        P(None, "head"),
        P(None, "head"),
        P("head", None),
    )
    out_specs = (
        P(None, "seq", None),
        P(None, "seq", None),
        P(),
        P("seq", "head", None),
        P(None, "head", None),
        P(),
        P(None, "head"),
        P("head"),
        P("seq", "head"),
        P(),
        P("head", "seq"),
        P(),
        P("seq", "head"),
        P("seq", "head"),
        P("head", "seq"),
    )
    return jax.shard_map(body, mesh=mesh, in_specs=in_specs, out_specs=out_specs, check_vma=False)
```

profile of v0, /device:TPU:0, one launch (start us, length us, event | category | flops | bytes accessed | tf_op | source)
XLA Modules:
  0.0 871.2 jit_solution(14256679517528602044)
XLA Ops:
  7.3 1.3 fusion.21
  9.2 1.9 fusion.35
  11.2 4.9 collective-permute-start
  19.1 1.2 convolution_bitcast_fusion.2
  20.4 4.3 while.58
  26.0 21.5 %all-gather.3 = f32[8,1,128]{2,1,0:T(1,128)S(1)} all-gather(f32[1,1,128]{2,1,0:T(1,128)S(1)} %get-tuple-element.555), channel_id=2, replica_groups=mesh['seq'=8,'head'=4] {'seq'}, dimensions={0}, use_global_device_ids=true | all-gather | bytes 4608 | tf_op jit(solution)/shard_map/all_gather | solution.py:20
  49.4 18.3 %all-gather.7.cloned.1.call-done = f32[8,128,256]{2,1,0:T(8,128)} async-done(((f32[1,128,256]{2,1,0:T(8,128)}), f32[8,128,256]{2,1,0:T(8,128)}) %all-gather.7.cloned.1.call-update) | async-done | bytes 1048592 | tf_op jit(solution)/shard_map/all_gather | solution.py:20
  67.7 7.3 while.59
  75.6 1.6 multiply_reduce_fusion.7
  77.3 2.2 multiply_convert_fusion.6
  79.4 1.3 fusion.118
  80.8 35.1 %all-reduce.7.cloned.1.call-done = f32[256,1024]{1,0:T(8,128)} async-done(((f32[256,1024]{1,0:T(8,128)}), f32[256,1024]{1,0:T(8,128)}) %all-reduce.7.cloned.1.call-update) | async-done | bytes 1048592 | tf_op jit(solution)/shard_map/psum | solution.py:161
  115.9 1.4 multiply_reduce_fusion.2
  121.3 1.5 multiply_convert_fusion.1
  123.6 1.6 convolution_add_fusion.2
  125.3 1.2 multiply_multiply_fusion.1
  126.5 35.6 %all-reduce.9.cloned.1.call-done = f32[256,1024]{1,0:T(8,128)} async-done(((f32[256,1024]{1,0:T(8,128)}), f32[256,1024]{1,0:T(8,128)}) %all-reduce.9.cloned.1.call-update) | async-done | bytes 1048592 | tf_op jit(solution)/shard_map/psum | solution.py:182
  162.1 2.2 multiply_reduce_fusion
  165.6 1.6 fusion.65
  168.0 1.2 convolution_bitcast_fusion.1
  170.1 9.2 %while.60 = (s32[]{:T(128)}, f32[1,128,256]{2,1,0:T(8,128)S(1)}, f32[4,1,128,256]{3,2,1,0:T(8,128)}, f32[4,1,128]{2,1,0:T(1,128)}, f32[4,1,128,256]{3,2,1,0:T(8,128)}, /*index=5*/s32[]{:T(128)}, s32[]{:T(128)}, s32[]{:T(128)}) while((s32[]{:T(128)}, f32[1,128,256]{2,1,0:T(8,128)S(1)}, f32[4,1,128,256]{3,2,1,0:T(8,128)}, ...), condition=%wide.region_15.16_spmd.clone, body=%wide.region_14.15_spmd.clone.sunk | while | flops 131076 | bytes 657016 | solution.py:87
  180.9 2.6 fusion.121
  187.3 33.6 %all-gather.9.cloned.1.call-done = f32[8,128,256]{2,1,0:T(8,128)} async-done(((f32[1,128,256]{2,1,0:T(8,128)}), f32[8,128,256]{2,1,0:T(8,128)}) %all-gather.9.cloned.1.call-update) | async-done | bytes 1048592 | tf_op jit(solution)/shard_map/all_gather | solution.py:20
  220.9 2.3 reverse_bitcast_fusion
  223.2 15.3 %while.61 = (s32[]{:T(128)}, f32[1,128,256]{2,1,0:T(8,128)S(1)}, s32[]{:T(128)}, f32[8,1,128]{2,1,0:T(1,128)}, f32[8,1,128,256]{3,2,1,0:T(8,128)}, /*index=5*/s32[]{:T(128)}, s32[]{:T(128)}) while((s32[]{:T(128)}, f32[1,128,256]{2,1,0:T(8,128)S(1)}, s32[]{:T(128)}, f32[8,1,128]{2,1,0:T(1,128)}, f32[8,1,128,256]{3,2,1,0:T(8,128)}, ...), condition=%wide.region_17.18_spmd.clone, body=%wide.region_16.17_spmd.clone.sunk | while | flops 131076 | bytes 394857 | solution.py:32
  239.5 1.8 convolution_add_fusion.3
  243.0 1.4 collective-permute-start.1
  246.1 2.6 collective-permute-done.1
  250.2 1.3 convolution_add_fusion
  251.6 1.9 convolution_bitcast_fusion
  254.5 2.6 fusion.70
  257.2 2.4 fusion.105
  259.6 3.1 fusion.124
  262.8 3.2 fusion.125
  267.0 3.2 fusion.51
  270.8 38.8 %psum.86 = f32[256]{0:T(256)} all-reduce(f32[256]{0:T(256)S(1)} %copy-done.89), channel_id=1, replica_groups=mesh['seq'=8,'head'=4] {'seq','head'}, use_global_device_ids=true, to_apply=%region_35.36 | all-reduce | flops 256 | bytes 2048 | tf_op jit(solution)/shard_map/psum | solution.py:263
  309.9 1.5 fusion.30
  311.4 37.7 %all-reduce = (f32[1024]{0:T(1024)}, f32[4,1,512]{2,1,0:T(1,128)}, f32[16,128]{1,0:T(8,128)}, f32[128]{0:T(128)}, f32[1024]{0:T(1024)}) all-reduce(f32[1024]{0:T(1024)S(1)} %get-tuple-element.475, f32[4,1,512]{2,1,0:T(1,128)S(1)} %reshape.447, f32[16,128]{1,0:T(8,128)S(1)} %fusion.99, ...), channel_id=1, replica_groups=mesh['seq'=8,'head'=4] {'seq'}, use_global_device_ids=true, to_apply=%region_22.23 | all-reduce | flops 6272 | bytes 50176 | tf_op jit(solution)/shard_map/psum | solution.py:262
  349.1 3.4 fusion.27
  352.5 21.5 %reduce-scatter.7.cloned.1.call-done = f32[128,1,512]{2,0,1:T(8,128)} async-done(((f32[1024,1,512]{2,0,1:T(8,128)}), f32[128,1,512]{2,0,1:T(8,128)}) %reduce-scatter.7.cloned.1.call-update) | async-done | bytes 262160 | tf_op jit(solution)/shard_map/reduce_scatter | solution.py:257
  374.1 1.9 copy.47
  376.0 122.0 %all-reduce.11.cloned.1.call-done = f32[1024,16]{0,1:T(8,128)} async-done(((f32[1024,16]{0,1:T(8,128)}), f32[1024,16]{0,1:T(8,128)}) %all-reduce.11.cloned.1.call-update) | async-done | bytes 65552 | tf_op jit(solution)/shard_map/psum | solution.py:263
  498.0 69.9 %reduce-scatter.11.cloned.1.call-done = f32[256,128]{1,0:T(8,128)} async-done(((f32[256,1024]{1,0:T(8,128)}), f32[256,128]{1,0:T(8,128)}) %reduce-scatter.11.cloned.1.call-update) | async-done | bytes 131088 | tf_op jit(solution)/shard_map/reduce_scatter | solution.py:259
  567.9 67.2 %reduce-scatter.9.cloned.1.call-done = f32[128,256]{1,0:T(8,128)} async-done(((f32[1024,256]{1,0:T(8,128)}), f32[128,256]{1,0:T(8,128)}) %reduce-scatter.9.cloned.1.call-update) | async-done | bytes 131088 | tf_op jit(solution)/shard_map/reduce_scatter | solution.py:258
  635.2 75.6 %reduce-scatter.13.cloned.1.call-done = f32[128,704]{0,1:T(8,128)} async-done(((f32[1024,704]{0,1:T(8,128)}), f32[128,704]{0,1:T(8,128)}) %reduce-scatter.13.cloned.1.call-update) | async-done | bytes 360464 | tf_op jit(solution)/shard_map/reduce_scatter | solution.py:178
  710.8 76.2 %reduce-scatter.15.cloned.1.call-done = f32[128,704]{0,1:T(8,128)} async-done(((f32[1024,704]{0,1:T(8,128)}), f32[128,704]{0,1:T(8,128)}) %reduce-scatter.15.cloned.1.call-update) | async-done | bytes 360464 | tf_op jit(solution)/shard_map/reduce_scatter | solution.py:179
  787.0 75.9 %reduce-scatter.17.cloned.1.call-done = f32[704,128]{1,0:T(8,128)} async-done(((f32[704,1024]{1,0:T(8,128)}), f32[704,128]{1,0:T(8,128)}) %reduce-scatter.17.cloned.1.call-update) | async-done | bytes 360464 | tf_op jit(solution)/shard_map/reduce_scatter | solution.py:180
  862.9 1.5 copy.89
  (319 shorter events, 64.4 us)
Async XLA Ops:
  7.2 113.7 %copy-start = (bf16[704,1024]{1,0:T(8,128)(2,1)S(1)}, bf16[704,1024]{1,0:T(8,128)(2,1)}, u32[]{:S(2)}) copy-start(bf16[704,1024]{1,0:T(8,128)(2,1)} %param.37) | copy-start | bytes 4325380
  7.2 8.9 %copy-start.3 = (bf16[1,256,1024]{2,1,0:T(8,128)(2,1)S(1)}, bf16[1,256,1024]{2,1,0:T(8,128)(2,1)}, u32[]{:S(2)}) copy-start(bf16[1,256,1024]{2,1,0:T(8,128)(2,1)} %param.23) | copy-start | bytes 1572868
  7.2 8.9 %copy-start.53 = (f32[1024]{0:T(1024)S(1)}, f32[1024]{0:T(1024)}, u32[]{:S(2)}) copy-start(f32[1024]{0:T(1024)} %param.25) | copy-start | bytes 12292
  7.2 8.9 %copy-start.55 = (bf16[1024,16]{0,1:T(8,128)(2,1)S(1)}, bf16[1024,16]{0,1:T(8,128)(2,1)}, u32[]{:S(2)}) copy-start(bf16[1024,16]{0,1:T(8,128)(2,1)} %param.28) | copy-start | bytes 98308
  7.2 60.5 %all-gather.7.cloned.1.call-start = ((), (), s32[]{:S(2)}) async-start(), calls=%async_computation.15 | async-start | bytes 1179648 | tf_op jit(solution)/shard_map/all_gather | solution.py:20
  9.2 7.2 copy-start.83
  9.2 7.2 copy-start.91
  9.2 8.2 copy-start.81
  11.2 7.5 copy-start.8
  11.2 6.3 collective-permute-start
  18.7 49.0 %copy-start.12 = (f32[1,256,128]{2,1,0:T(8,128)}, f32[1,256,128]{2,1,0:T(8,128)S(1)}, u32[]{:S(2)}) copy-start(f32[1,256,128]{2,1,0:T(8,128)S(1)} %slice.81) | copy-start | bytes 393220
  18.8 29.7 %copy-start.19 = (bf16[1,256,256]{2,1,0:T(8,128)(2,1)}, bf16[1,256,256]{2,1,0:T(8,128)(2,1)S(1)}, u32[]{:S(2)}) copy-start(bf16[1,256,256]{2,1,0:T(8,128)(2,1)S(1)} %slice.82) | copy-start | bytes 393220
  19.1 148.3 %copy-start.24 = (f32[1,4,64,128]{3,2,1,0:T(8,128)}, f32[1,4,64,128]{3,2,1,0:T(8,128)S(1)}, u32[]{:S(2)}) copy-start(f32[1,4,64,128]{3,2,1,0:T(8,128)S(1)} %get-tuple-element.558) | copy-start | bytes 393220
  24.7 50.9 %copy-start.16 = (f32[4,1,128,256]{3,2,1,0:T(8,128)}, f32[4,1,128,256]{3,2,1,0:T(8,128)S(1)}, u32[]{:S(2)}) copy-start(f32[4,1,128,256]{3,2,1,0:T(8,128)S(1)} %get-tuple-element.335) | copy-start | bytes 1572868
  25.3 90.6 %all-reduce.7.cloned.1.call-start = ((), (), s32[]{:S(2)}) async-start(), calls=%async_computation.6 | async-start | bytes 2097152 | tf_op jit(solution)/shard_map/psum | solution.py:161
  25.4 42.3 %copy-start.47 = (f32[64,64]{1,0:T(8,128)}, f32[64,64]{1,0:T(8,128)S(1)}, u32[]{:S(2)}) copy-start(f32[64,64]{1,0:T(8,128)S(1)} %fusion.102) | copy-start | bytes 49156
  48.1 27.5 %copy-start.60 = (f32[4,128]{1,0:T(4,128)}, f32[4,128]{1,0:T(4,128)S(1)}, u32[]{:S(2)}) copy-start(f32[4,128]{1,0:T(4,128)S(1)} %get-tuple-element.549) | copy-start | bytes 6148
  48.5 28.7 %copy-start.34 = (f32[4,64,64]{2,1,0:T(8,128)}, f32[4,64,64]{2,1,0:T(8,128)S(1)}, u32[]{:S(2)}) copy-start(f32[4,64,64]{2,1,0:T(8,128)S(1)} %convolution_multiply_fusion.1) | copy-start | bytes 196612
  67.7 9.6 %copy-start.87 = (f32[256]{0:T(256)S(1)}, f32[256]{0:T(256)}, u32[]{:S(2)}) copy-start(f32[256]{0:T(256)} %param.32) | copy-start | bytes 3076
  80.7 37.2 %copy-start.54 = (f32[1024]{0:T(1024)S(1)}, f32[1024]{0:T(1024)}, u32[]{:S(2)}) copy-start(f32[1024]{0:T(1024)} %param.34) | copy-start | bytes 12292
  80.8 81.4 %all-reduce.9.cloned.1.call-start = ((), (), s32[]{:S(2)}) async-start(), calls=%async_computation.7 | async-start | bytes 2097152 | tf_op jit(solution)/shard_map/psum | solution.py:182
  125.2 95.7 %all-gather.9.cloned.1.call-start = ((), (), s32[]{:S(2)}) async-start(), calls=%async_computation.16 | async-start | bytes 1179648 | tf_op jit(solution)/shard_map/all_gather | solution.py:20
  170.1 10.1 %copy-start.73 = (f32[8,1,128]{2,1,0:T(1,128)S(1)}, f32[8,1,128]{2,1,0:T(1,128)}, u32[]{:S(2)}) copy-start(f32[8,1,128]{2,1,0:T(1,128)} %copy-done.72) | copy-start | bytes 12292
  180.0 129.8 %all-reduce.13.cloned.1.call-start = ((), (), s32[]{:S(2)}) async-start(), calls=%async_computation.17 | async-start | bytes 4194304 | tf_op jit(solution)/shard_map/psum | solution.py:168
  223.2 15.4 %copy-start.2 = (f32[1,128,256]{2,1,0:T(8,128)S(1)}, f32[1,128,256]{2,1,0:T(8,128)}, u32[]{:S(2)}) copy-start(f32[1,128,256]{2,1,0:T(8,128)} %copy-done.1) | copy-start | bytes 393220
  223.2 16.3 %copy-start.59 = (f32[4,128]{1,0:T(4,128)S(1)}, f32[4,128]{1,0:T(4,128)}, u32[]{:S(2)}) copy-start(f32[4,128]{1,0:T(4,128)} %get-tuple-element.548) | copy-start | bytes 6148
  242.0 4.0 copy-start.84
  242.0 6.7 copy-start.63
  242.0 6.7 copy-start.65
  242.0 6.7 copy-start.67
  242.0 6.7 copy-start.69
  243.0 5.9 copy-start.38
  243.0 5.7 collective-permute-start.1
  251.5 122.5 %reduce-scatter.7.cloned.1.call-start = ((), (), s32[]{:S(2)}) async-start(), calls=%async_computation.8 | async-start | bytes 2359296 | tf_op jit(solution)/shard_map/reduce_scatter | solution.py:257
  253.5 244.6 %all-reduce.11.cloned.1.call-start = ((), (), s32[]{:S(2)}) async-start(), calls=%async_computation.9 | async-start | bytes 131072 | tf_op jit(solution)/shard_map/psum | solution.py:263
  254.5 313.5 %reduce-scatter.11.cloned.1.call-start = ((), (), s32[]{:S(2)}) async-start(), calls=%async_computation.11 | async-start | bytes 1179648 | tf_op jit(solution)/shard_map/reduce_scatter | solution.py:259
  257.1 378.0 %reduce-scatter.9.cloned.1.call-start = ((), (), s32[]{:S(2)}) async-start(), calls=%async_computation.10 | async-start | bytes 1179648 | tf_op jit(solution)/shard_map/reduce_scatter | solution.py:258
  259.6 451.2 %reduce-scatter.13.cloned.1.call-start = ((), (), s32[]{:S(2)}) async-start(), calls=%async_computation.12 | async-start | bytes 3244032 | tf_op jit(solution)/shard_map/reduce_scatter | solution.py:178
  262.7 524.2 %reduce-scatter.15.cloned.1.call-start = ((), (), s32[]{:S(2)}) async-start(), calls=%async_computation.13 | async-start | bytes 3244032 | tf_op jit(solution)/shard_map/reduce_scatter | solution.py:179
  266.0 596.9 %reduce-scatter.17.cloned.1.call-start = ((), (), s32[]{:S(2)}) async-start(), calls=%async_computation.14 | async-start | bytes 3244032 | tf_op jit(solution)/shard_map/reduce_scatter | solution.py:180
  270.2 39.5 %copy-start.76 = (f32[512]{0:T(512)S(1)}, f32[512]{0:T(512)}, u32[]{:S(2)}) copy-start(f32[512]{0:T(512)} %get-tuple-element.478) | copy-start | bytes 6148
  270.2 39.5 %copy-start.77 = (f32[512]{0:T(512)S(1)}, f32[512]{0:T(512)}, u32[]{:S(2)}) copy-start(f32[512]{0:T(512)} %get-tuple-element.479) | copy-start | bytes 6148
  270.2 39.5 %copy-start.78 = (f32[512]{0:T(512)S(1)}, f32[512]{0:T(512)}, u32[]{:S(2)}) copy-start(f32[512]{0:T(512)} %get-tuple-element.482) | copy-start | bytes 6148
  270.2 39.5 %copy-start.51 = (bf16[256,128]{1,0:T(8,128)(2,1)S(1)}, bf16[256,128]{1,0:T(8,128)(2,1)}, u32[]{:S(2)}) copy-start(bf16[256,128]{1,0:T(8,128)(2,1)} %copy-done.50) | copy-start | bytes 196612
  270.2 39.5 %copy-start.80 = (bf16[256,16]{0,1:T(8,128)(2,1)S(1)}, bf16[256,16]{0,1:T(8,128)(2,1)}, u32[]{:S(2)}) copy-start(bf16[256,16]{0,1:T(8,128)(2,1)} %copy-done.79) | copy-start | bytes 24580
  270.2 41.2 %copy-start.71 = (f32[1024]{0:T(1024)S(1)}, f32[1024]{0:T(1024)}, u32[]{:S(2)}) copy-start(f32[1024]{0:T(1024)} %get-tuple-element.473) | copy-start | bytes 12292
  270.2 41.2 %copy-start.90 = (f32[128]{0:T(128)S(1)}, f32[128]{0:T(128)}, u32[]{:S(2)}) copy-start(f32[128]{0:T(128)} %get-tuple-element.566) | copy-start | bytes 1540
  270.2 78.9 %copy-start.85 = (f32[256]{0:T(256)S(1)}, f32[256]{0:T(256)}, u32[]{:S(2)}) copy-start(f32[256]{0:T(256)} %get-tuple-element.550) | copy-start | bytes 3076
  (59 other events, 104.7 us)
Sparse Core Ops, SparseCore 0:
  25.4 42.2 all-gather.6
  80.9 34.9 all-reduce.6
  125.4 36.7 all-reduce.8
  180.1 40.7 all-gather.8
  251.6 50.4 all-reduce.12
  305.5 68.4 reduce-scatter.6
  379.6 118.3 all-reduce.10
  502.0 65.8 reduce-scatter.10
  571.9 63.1 reduce-scatter.8
  639.1 71.6 reduce-scatter.12
  714.9 71.9 reduce-scatter.14
  791.0 71.8 reduce-scatter.16
where the time goes:
time: 873 us; the launch traced here: 871 us
  waiting for transfers between devices  634 us (73%)
  blocking collectives  98 us (11%)
  matrix products  47.6 us (5%)
  other arithmetic  42.4 us (5%)
  local copies, waits for them, and re-layouts  26.4 us (3%)
  between operations  15.4 us (2%)
    psum x1, waiting for transfers between devices, body(): shared = lax.psum((grad_scale, grad_squeeze), ('seq', 'head'))  122 us
    reduce_scatter x1, waiting for transfers between devices, body(): lax.psum_scatter(grad_lift, 'seq', scatter_dimension=0, tiled=True)  76.2 us
    reduce_scatter x1, waiting for transfers between devices, body(): lax.psum_scatter(grad_drop, 'seq', scatter_dimension=1, tiled=True)  75.9 us
    reduce_scatter x1, waiting for transfers between devices, body(): lax.psum_scatter(grad_gate, 'seq', scatter_dimension=0, tiled=True)  75.6 us
    reduce_scatter x1, waiting for transfers between devices, body(): lax.psum_scatter(grad_output, 'seq', scatter_dimension=1, tiled=True)  69.9 us
    reduce_scatter x1, waiting for transfers between devices, body(): lax.psum_scatter(grad_gating, 'seq', scatter_dimension=0, tiled=True)  67.2 us
    all_gather x2, waiting for transfers between devices, entering(): pieces = jax.tree.map(lambda part: lax.all_gather(part, axis), value)  51.9 us
    psum x1, blocking collectives, body(): shared = lax.psum((grad_scale, grad_squeeze), ('seq', 'head'))  38.8 us
  transfers between devices with their start and end apart: 14, of which 12 were waited for; matrix products, arithmetic and copies ran while one was open for 4% of the time, Pallas kernels for 0%

commit v1 on v0

--- a/solution.py
+++ b/solution.py
@@ -260,7 +260,7 @@
     )
     summed = tuple(mixer_grads) + tuple(feed_grads)
     small_head = lax.psum((grad_taps, grad_expand, grad_bias, grad_first, grad_second), "seq")
-    shared = lax.psum((grad_scale, grad_squeeze), ("seq", "head"))
+    shared = lax.psum(lax.psum((grad_scale, grad_squeeze), "seq"), "head")
     return (
         block_out,
         input_grad,

time: 873 us -> 817 us (0.936)
  blocking collectives: 98 us -> 66 us
  waiting for transfers between devices: 634 us -> 606 us
    psum x1, waiting for transfers between devices: 122 us -> 61 us  [body(): shared = lax.psum(lax.psum((grad_scale, grad_squeeze), 'seq'), 'head')]
    psum x1, waiting for transfers between devices: 0.01 us -> 35.4 us  [body(): feed = lax.psum(product(inner, hidden_drop), 'head')]
    psum x1, blocking collectives: 38.8 us -> 6.43 us  [body(): shared = lax.psum(lax.psum((grad_scale, grad_squeeze), 'seq'), 'head')]
  transfers between devices with their start and end apart: 14 -> 14, of which waited for: 12 -> 13; matrix products, arithmetic and copies ran while one was open for 4% -> 5% of each run, Pallas kernels for 0% -> 0%
where the time goes in v1:
time: 817 us; the launch traced here: 815 us
  waiting for transfers between devices  606 us (74%)
  blocking collectives  66 us (8%)
  matrix products  48.8 us (6%)
  other arithmetic  44.4 us (5%)
  local copies, waits for them, and re-layouts  27.2 us (3%)
  between operations  15.3 us (2%)
    reduce_scatter x1, waiting for transfers between devices, body(): lax.psum_scatter(grad_lift, 'seq', scatter_dimension=0, tiled=True)  76.3 us
    reduce_scatter x1, waiting for transfers between devices, body(): lax.psum_scatter(grad_drop, 'seq', scatter_dimension=1, tiled=True)  76.1 us
    reduce_scatter x1, waiting for transfers between devices, body(): lax.psum_scatter(grad_gate, 'seq', scatter_dimension=0, tiled=True)  76 us
    reduce_scatter x1, waiting for transfers between devices, body(): lax.psum_scatter(grad_gating, 'seq', scatter_dimension=0, tiled=True)  67.1 us
    reduce_scatter x1, waiting for transfers between devices, body(): lax.psum_scatter(grad_output, 'seq', scatter_dimension=1, tiled=True)  65.8 us
    psum x1, waiting for transfers between devices, body(): shared = lax.psum(lax.psum((grad_scale, grad_squeeze), 'seq'), 'head')  61 us
    all_gather x2, waiting for transfers between devices, entering(): pieces = jax.tree.map(lambda part: lax.all_gather(part, axis), value)  51.8 us
    psum x1, blocking collectives, body(): lax.psum((grad_taps, grad_expand, grad_bias, grad_first, grad_second), 's...  38 us
  transfers between devices with their start and end apart: 14, of which 13 were waited for; matrix products, arithmetic and copies ran while one was open for 5% of the time, Pallas kernels for 0%

profile of v1, /device:TPU:0, one launch (start us, length us, event | category | flops | bytes accessed | tf_op | source)
XLA Modules:
  0.0 815.3 jit_solution(5803230161805368193)
XLA Ops:
  7.3 1.3 fusion.21
  9.2 1.9 fusion.35
  11.2 4.9 collective-permute-start
  19.1 1.2 convolution_bitcast_fusion.2
  20.3 4.3 while.58
  26.0 21.5 %all-gather.3 = f32[8,1,128]{2,1,0:T(1,128)S(1)} all-gather(f32[1,1,128]{2,1,0:T(1,128)S(1)} %get-tuple-element.557), channel_id=2, replica_groups=mesh['seq'=8,'head'=4] {'seq'}, dimensions={0}, use_global_device_ids=true | all-gather | bytes 4608 | tf_op jit(solution)/shard_map/all_gather | solution.py:20
  49.5 18.2 %all-gather.7.cloned.1.call-done = f32[8,128,256]{2,1,0:T(8,128)} async-done(((f32[1,128,256]{2,1,0:T(8,128)}), f32[8,128,256]{2,1,0:T(8,128)}) %all-gather.7.cloned.1.call-update) | async-done | bytes 1048592 | tf_op jit(solution)/shard_map/all_gather | solution.py:20
  67.7 7.3 while.59
  75.6 1.6 multiply_reduce_fusion.7
  77.2 2.2 multiply_convert_fusion.6
  79.4 1.3 fusion.118
  80.8 35.1 %all-reduce.7.cloned.1.call-done = f32[256,1024]{1,0:T(8,128)} async-done(((f32[256,1024]{1,0:T(8,128)}), f32[256,1024]{1,0:T(8,128)}) %all-reduce.7.cloned.1.call-update) | async-done | bytes 1048592 | tf_op jit(solution)/shard_map/psum | solution.py:161
  115.9 1.4 multiply_reduce_fusion.2
  121.3 1.5 multiply_convert_fusion.1
  123.6 1.6 convolution_add_fusion.2
  126.5 35.6 %all-reduce.9.cloned.1.call-done = f32[256,1024]{1,0:T(8,128)} async-done(((f32[256,1024]{1,0:T(8,128)}), f32[256,1024]{1,0:T(8,128)}) %all-reduce.9.cloned.1.call-update) | async-done | bytes 1048592 | tf_op jit(solution)/shard_map/psum | solution.py:182
  162.1 2.2 multiply_reduce_fusion
  165.6 1.6 fusion.65
  170.1 9.3 %while.60 = (s32[]{:T(128)}, f32[1,128,256]{2,1,0:T(8,128)S(1)}, f32[4,1,128,256]{3,2,1,0:T(8,128)}, f32[4,1,128]{2,1,0:T(1,128)}, f32[4,1,128,256]{3,2,1,0:T(8,128)}, /*index=5*/s32[]{:T(128)}, s32[]{:T(128)}, s32[]{:T(128)}) while((s32[]{:T(128)}, f32[1,128,256]{2,1,0:T(8,128)S(1)}, f32[4,1,128,256]{3,2,1,0:T(8,128)}, ...), condition=%wide.region_15.16_spmd.clone, body=%wide.region_14.15_spmd.clone.sunk | while | flops 131076 | bytes 657016 | solution.py:87
  180.9 2.6 fusion.121
  187.4 33.6 %all-gather.9.cloned.1.call-done = f32[8,128,256]{2,1,0:T(8,128)} async-done(((f32[1,128,256]{2,1,0:T(8,128)}), f32[8,128,256]{2,1,0:T(8,128)}) %all-gather.9.cloned.1.call-update) | async-done | bytes 1048592 | tf_op jit(solution)/shard_map/all_gather | solution.py:20
  221.0 2.3 reverse_bitcast_fusion
  223.3 15.3 %while.61 = (s32[]{:T(128)}, f32[1,128,256]{2,1,0:T(8,128)S(1)}, s32[]{:T(128)}, f32[8,1,128]{2,1,0:T(1,128)}, f32[8,1,128,256]{3,2,1,0:T(8,128)}, /*index=5*/s32[]{:T(128)}, s32[]{:T(128)}) while((s32[]{:T(128)}, f32[1,128,256]{2,1,0:T(8,128)S(1)}, s32[]{:T(128)}, f32[8,1,128]{2,1,0:T(1,128)}, f32[8,1,128,256]{3,2,1,0:T(8,128)}, ...), condition=%wide.region_17.18_spmd.clone, body=%wide.region_16.17_spmd.clone.sunk | while | flops 131076 | bytes 394857 | solution.py:32
  239.6 1.7 convolution_add_fusion.3
  245.4 1.3 collective-permute-start.1
  247.7 3.2 collective-permute-done.1
  250.9 2.1 fusion.42
  253.0 1.7 fusion.33
  255.5 1.3 convolution_add_fusion
  256.8 61.0 %all-reduce.11.cloned.1.call-done = f32[1024,16]{0,1:T(8,128)} async-done(((f32[1024,16]{0,1:T(8,128)}), f32[1024,16]{0,1:T(8,128)}) %all-reduce.11.cloned.1.call-update) | async-done | bytes 65552 | tf_op jit(solution)/shard_map/psum | solution.py:263
  317.9 1.9 convolution_bitcast_fusion
  320.6 2.5 fusion.70
  323.3 2.4 fusion.105
  325.7 3.1 fusion.124
  328.9 3.1 fusion.125
  333.1 3.2 fusion.51
  337.2 35.4 %all-reduce.13.cloned.1.call-done = (f32[256,1024]{1,0:T(8,128)}, f32[256,1024]{1,0:T(8,128)}, f32[1024,16]{0,1:T(8,128)}) async-done(((f32[256,1024]{1,0:T(8,128)}, f32[256,1024]{1,0:T(8,128)}, f32[1024,16]{0,1:T(8,128)}), (f32[256,1024]{1,0:T(8,128)}, f32[256,1024]{1,0:T(8,128)}, f32[1024,16]{0,1:T(8,128)})) %all-reduce.13.cloned.1.call-update) | async-done | bytes 2162704 | tf_op jit(solution)/shard_map/psum | solution.py:168
  372.6 1.5 fusion.30
  374.2 38.0 %all-reduce = (f32[1024]{0:T(1024)}, f32[4,1,512]{2,1,0:T(1,128)}, f32[16,128]{1,0:T(8,128)}, f32[128]{0:T(128)}, f32[256]{0:T(256)S(1)}, /*index=5*/f32[1024]{0:T(1024)}) all-reduce(f32[1024]{0:T(1024)S(1)} %get-tuple-element.475, f32[4,1,512]{2,1,0:T(1,128)S(1)} %reshape.447, ...), channel_id=1, replica_groups=mesh['seq'=8,'head'=4] {'seq'}, use_global_device_ids=true, to_apply=%region_22.23 | all-reduce | flops 6528 | bytes 52224 | tf_op jit(solution)/shard_map/psum | solution.py:262
  412.2 6.4 psum.102
  418.7 3.5 fusion.27
  422.1 22.5 %reduce-scatter.7.cloned.1.call-done = f32[128,1,512]{2,0,1:T(8,128)} async-done(((f32[1024,1,512]{2,0,1:T(8,128)}), f32[128,1,512]{2,0,1:T(8,128)}) %reduce-scatter.7.cloned.1.call-update) | async-done | bytes 262160 | tf_op jit(solution)/shard_map/reduce_scatter | solution.py:257
  444.6 1.9 copy.47
  446.5 65.8 %reduce-scatter.11.cloned.1.call-done = f32[256,128]{1,0:T(8,128)} async-done(((f32[256,1024]{1,0:T(8,128)}), f32[256,128]{1,0:T(8,128)}) %reduce-scatter.11.cloned.1.call-update) | async-done | bytes 131088 | tf_op jit(solution)/shard_map/reduce_scatter | solution.py:259
  512.3 67.1 %reduce-scatter.9.cloned.1.call-done = f32[128,256]{1,0:T(8,128)} async-done(((f32[1024,256]{1,0:T(8,128)}), f32[128,256]{1,0:T(8,128)}) %reduce-scatter.9.cloned.1.call-update) | async-done | bytes 131088 | tf_op jit(solution)/shard_map/reduce_scatter | solution.py:258
  579.4 76.0 %reduce-scatter.13.cloned.1.call-done = f32[128,704]{0,1:T(8,128)} async-done(((f32[1024,704]{0,1:T(8,128)}), f32[128,704]{0,1:T(8,128)}) %reduce-scatter.13.cloned.1.call-update) | async-done | bytes 360464 | tf_op jit(solution)/shard_map/reduce_scatter | solution.py:178
  655.4 76.3 %reduce-scatter.15.cloned.1.call-done = f32[128,704]{0,1:T(8,128)} async-done(((f32[1024,704]{0,1:T(8,128)}), f32[128,704]{0,1:T(8,128)}) %reduce-scatter.15.cloned.1.call-update) | async-done | bytes 360464 | tf_op jit(solution)/shard_map/reduce_scatter | solution.py:179
  731.7 76.1 %reduce-scatter.17.cloned.1.call-done = f32[704,128]{1,0:T(8,128)} async-done(((f32[704,1024]{1,0:T(8,128)}), f32[704,128]{1,0:T(8,128)}) %reduce-scatter.17.cloned.1.call-update) | async-done | bytes 360464 | tf_op jit(solution)/shard_map/reduce_scatter | solution.py:180
  (321 shorter events, 68.6 us)
Async XLA Ops:
  7.2 113.6 %copy-start = (bf16[704,1024]{1,0:T(8,128)(2,1)S(1)}, bf16[704,1024]{1,0:T(8,128)(2,1)}, u32[]{:S(2)}) copy-start(bf16[704,1024]{1,0:T(8,128)(2,1)} %param.37) | copy-start | bytes 4325380
  7.2 8.9 %copy-start.3 = (bf16[1,256,1024]{2,1,0:T(8,128)(2,1)S(1)}, bf16[1,256,1024]{2,1,0:T(8,128)(2,1)}, u32[]{:S(2)}) copy-start(bf16[1,256,1024]{2,1,0:T(8,128)(2,1)} %param.23) | copy-start | bytes 1572868
  7.2 8.9 %copy-start.54 = (f32[1024]{0:T(1024)S(1)}, f32[1024]{0:T(1024)}, u32[]{:S(2)}) copy-start(f32[1024]{0:T(1024)} %param.25) | copy-start | bytes 12292
  7.2 8.9 %copy-start.56 = (bf16[1024,16]{0,1:T(8,128)(2,1)S(1)}, bf16[1024,16]{0,1:T(8,128)(2,1)}, u32[]{:S(2)}) copy-start(bf16[1024,16]{0,1:T(8,128)(2,1)} %param.28) | copy-start | bytes 98308
  7.2 60.5 %all-gather.7.cloned.1.call-start = ((), (), s32[]{:S(2)}) async-start(), calls=%async_computation.15 | async-start | bytes 1179648 | tf_op jit(solution)/shard_map/all_gather | solution.py:20
  9.2 7.2 copy-start.84
  9.2 7.2 copy-start.92
  9.2 8.2 %copy-start.82 = (f32[4,1,512]{2,1,0:T(1,128)S(1)}, f32[4,1,512]{2,1,0:T(1,128)}, u32[]{:S(2)}) copy-start(f32[4,1,512]{2,1,0:T(1,128)} %param.27) | copy-start | bytes 24580
  11.1 7.4 copy-start.8
  11.2 6.3 collective-permute-start
  18.7 49.0 %copy-start.12 = (f32[1,256,128]{2,1,0:T(8,128)}, f32[1,256,128]{2,1,0:T(8,128)S(1)}, u32[]{:S(2)}) copy-start(f32[1,256,128]{2,1,0:T(8,128)S(1)} %slice.81) | copy-start | bytes 393220
  18.7 29.7 %copy-start.19 = (bf16[1,256,256]{2,1,0:T(8,128)(2,1)}, bf16[1,256,256]{2,1,0:T(8,128)(2,1)S(1)}, u32[]{:S(2)}) copy-start(bf16[1,256,256]{2,1,0:T(8,128)(2,1)S(1)} %slice.82) | copy-start | bytes 393220
  19.0 148.4 %copy-start.24 = (f32[1,4,64,128]{3,2,1,0:T(8,128)}, f32[1,4,64,128]{3,2,1,0:T(8,128)S(1)}, u32[]{:S(2)}) copy-start(f32[1,4,64,128]{3,2,1,0:T(8,128)S(1)} %get-tuple-element.560) | copy-start | bytes 393220
  24.6 50.9 %copy-start.16 = (f32[4,1,128,256]{3,2,1,0:T(8,128)}, f32[4,1,128,256]{3,2,1,0:T(8,128)S(1)}, u32[]{:S(2)}) copy-start(f32[4,1,128,256]{3,2,1,0:T(8,128)S(1)} %get-tuple-element.335) | copy-start | bytes 1572868
  25.3 90.6 %all-reduce.7.cloned.1.call-start = ((), (), s32[]{:S(2)}) async-start(), calls=%async_computation.6 | async-start | bytes 2097152 | tf_op jit(solution)/shard_map/psum | solution.py:161
  25.4 42.3 %copy-start.47 = (f32[64,64]{1,0:T(8,128)}, f32[64,64]{1,0:T(8,128)S(1)}, u32[]{:S(2)}) copy-start(f32[64,64]{1,0:T(8,128)S(1)} %fusion.102) | copy-start | bytes 49156
  48.1 27.4 %copy-start.61 = (f32[4,128]{1,0:T(4,128)}, f32[4,128]{1,0:T(4,128)S(1)}, u32[]{:S(2)}) copy-start(f32[4,128]{1,0:T(4,128)S(1)} %get-tuple-element.551) | copy-start | bytes 6148
  48.5 28.6 %copy-start.35 = (f32[4,64,64]{2,1,0:T(8,128)}, f32[4,64,64]{2,1,0:T(8,128)S(1)}, u32[]{:S(2)}) copy-start(f32[4,64,64]{2,1,0:T(8,128)S(1)} %convolution_multiply_fusion.1) | copy-start | bytes 196612
  67.7 9.6 %copy-start.88 = (f32[256]{0:T(256)S(1)}, f32[256]{0:T(256)}, u32[]{:S(2)}) copy-start(f32[256]{0:T(256)} %param.32) | copy-start | bytes 3076
  80.7 37.2 %copy-start.55 = (f32[1024]{0:T(1024)S(1)}, f32[1024]{0:T(1024)}, u32[]{:S(2)}) copy-start(f32[1024]{0:T(1024)} %param.34) | copy-start | bytes 12292
  80.7 81.4 %all-reduce.9.cloned.1.call-start = ((), (), s32[]{:S(2)}) async-start(), calls=%async_computation.7 | async-start | bytes 2097152 | tf_op jit(solution)/shard_map/psum | solution.py:182
  125.2 95.8 %all-gather.9.cloned.1.call-start = ((), (), s32[]{:S(2)}) async-start(), calls=%async_computation.16 | async-start | bytes 1179648 | tf_op jit(solution)/shard_map/all_gather | solution.py:20
  170.1 10.2 %copy-start.74 = (f32[8,1,128]{2,1,0:T(1,128)S(1)}, f32[8,1,128]{2,1,0:T(1,128)}, u32[]{:S(2)}) copy-start(f32[8,1,128]{2,1,0:T(1,128)} %copy-done.73) | copy-start | bytes 12292
  180.1 3.5 copy-start.20
  180.1 137.7 %all-reduce.11.cloned.1.call-start = ((), (), s32[]{:S(2)}) async-start(), calls=%async_computation.9 | async-start | bytes 131072 | tf_op jit(solution)/shard_map/psum | solution.py:263
  180.9 2.9 copy-start.25
  180.9 3.9 copy-start.13
  223.3 15.4 %copy-start.2 = (f32[1,128,256]{2,1,0:T(8,128)S(1)}, f32[1,128,256]{2,1,0:T(8,128)}, u32[]{:S(2)}) copy-start(f32[1,128,256]{2,1,0:T(8,128)} %copy-done.1) | copy-start | bytes 393220
  223.3 16.3 %copy-start.60 = (f32[4,128]{1,0:T(4,128)S(1)}, f32[4,128]{1,0:T(4,128)}, u32[]{:S(2)}) copy-start(f32[4,128]{1,0:T(4,128)} %get-tuple-element.550) | copy-start | bytes 6148
  243.5 7.4 copy-start.64
  243.5 7.4 copy-start.66
  243.5 7.4 copy-start.68
  243.5 7.4 copy-start.70
  245.4 5.5 collective-permute-start.1
  247.6 7.1 copy-start.46
  247.6 125.0 %all-reduce.13.cloned.1.call-start = ((), (), s32[]{:S(2)}) async-start(), calls=%async_computation.17 | async-start | bytes 4325376 | tf_op jit(solution)/shard_map/psum | solution.py:168
  247.7 7.0 copy-start.43
  317.8 126.8 %reduce-scatter.7.cloned.1.call-start = ((), (), s32[]{:S(2)}) async-start(), calls=%async_computation.8 | async-start | bytes 2359296 | tf_op jit(solution)/shard_map/reduce_scatter | solution.py:257
  319.8 192.6 %reduce-scatter.11.cloned.1.call-start = ((), (), s32[]{:S(2)}) async-start(), calls=%async_computation.11 | async-start | bytes 1179648 | tf_op jit(solution)/shard_map/reduce_scatter | solution.py:259
  323.2 256.2 %reduce-scatter.9.cloned.1.call-start = ((), (), s32[]{:S(2)}) async-start(), calls=%async_computation.10 | async-start | bytes 1179648 | tf_op jit(solution)/shard_map/reduce_scatter | solution.py:258
  325.7 329.8 %reduce-scatter.13.cloned.1.call-start = ((), (), s32[]{:S(2)}) async-start(), calls=%async_computation.12 | async-start | bytes 3244032 | tf_op jit(solution)/shard_map/reduce_scatter | solution.py:178
  328.8 402.9 %reduce-scatter.15.cloned.1.call-start = ((), (), s32[]{:S(2)}) async-start(), calls=%async_computation.13 | async-start | bytes 3244032 | tf_op jit(solution)/shard_map/reduce_scatter | solution.py:179
  332.1 475.8 %reduce-scatter.17.cloned.1.call-start = ((), (), s32[]{:S(2)}) async-start(), calls=%async_computation.14 | async-start | bytes 3244032 | tf_op jit(solution)/shard_map/reduce_scatter | solution.py:180
  336.3 37.9 %copy-start.72 = (f32[1024]{0:T(1024)S(1)}, f32[1024]{0:T(1024)}, u32[]{:S(2)}) copy-start(f32[1024]{0:T(1024)} %get-tuple-element.473) | copy-start | bytes 12292
  336.3 37.9 %copy-start.90 = (f32[256]{0:T(256)S(1)}, f32[256]{0:T(256)}, u32[]{:S(2)}) copy-start(f32[256]{0:T(256)} %get-tuple-element.480) | copy-start | bytes 3076
  336.3 37.9 %copy-start.91 = (f32[128]{0:T(128)S(1)}, f32[128]{0:T(128)}, u32[]{:S(2)}) copy-start(f32[128]{0:T(128)} %get-tuple-element.568) | copy-start | bytes 1540
  336.3 82.3 %copy-start.86 = (f32[256]{0:T(256)S(1)}, f32[256]{0:T(256)}, u32[]{:S(2)}) copy-start(f32[256]{0:T(256)} %get-tuple-element.552) | copy-start | bytes 3076
  418.7 389.2 %copy-start.53 = (f32[1024,16]{0,1:T(8,128)S(1)}, f32[1024,16]{0,1:T(8,128)}, u32[]{:S(2)}) copy-start(f32[1024,16]{0,1:T(8,128)} %get-tuple-element.790) | copy-start | bytes 196612
  (60 other events, 92.0 us)
Sparse Core Ops, SparseCore 0:
  25.4 42.2 all-gather.6
  80.8 34.9 all-reduce.6
  125.3 36.7 all-reduce.8
  180.2 40.7 all-gather.8
  247.7 70.0 all-reduce.10
  320.2 52.4 all-reduce.12
  376.2 68.4 reduce-scatter.6
  448.6 63.6 reduce-scatter.10
  516.3 63.0 reduce-scatter.8
  583.4 71.9 reduce-scatter.12
  659.6 72.0 reduce-scatter.14
  735.7 72.0 reduce-scatter.16
